TPU v7x, 512 devices: a whole 4x4x16 slice. The times are simulated.
512 devices in a mesh: event: 8 (over y, core), tile: 64 (over x, z).
Axes of the slice: x: 4, y: 4, z: 16, core: 2. Of those that a mesh axis runs over, the one named last changes fastest.
Arguments:
- surface_start: float32 [8, 512, 8192], P('event', 'tile'), may hold values from -6 to 6
- east_start: float32 [8, 512, 8192], P('event', 'tile'), may hold values from -5 to 5
- north_start: float32 [8, 512, 8192], P('event', 'tile'), may hold values from -5 to 5
- still_depth: float32 [512, 8192], P('tile'), may hold values from 1 to 4
- roughness: float32 [512, 8192], P('tile'), may hold values from 0.5 to 2
- wet_masks: int32 [8, 2, 512, 8192], P('event', None, 'tile'), may hold values 0 or 1
- gauge_tiles: int32 [8, 16384, 1], P('event', 'tile'), may hold values from 0 to 63; in each aligned block of 256 rows (0 to 255, 256 to 511, ..., all dimensions but the last counted through in order) at most 8 rows name the same one
- gauge_cells: int32 [8, 16384], P('event', 'tile'), may hold values from 0 to 65535
- gauge_values: float32 [8, 16384], P('event', 'tile'), may hold values from -6 to 6
- survey_surface: float32 [8, 512, 8192], P('event', 'tile'), may hold values from -6 to 6
Outputs:
- roughness_grad: float32 [512, 8192], P('tile', 'event')
Inputs may be any that keep to these rules, and one draw needn't show every extreme that they name: `gauge_tiles`: of the gauges of one event listed on one strip, at most 8 lie in any one strip, and some strip receives exactly 8.
All inputs are finite; a program needn't handle non-finite values. No bound on the sum of `wet_masks` on one device may be relied on, other than what follows from the above.
Results may differ from a plain program's by a relative error of at most 0.0003.
Values sent between devices are 32-bit elements; how exact they have to be, the bound alone decides.
No kernel may reach another device: no remote copies, remote signals or barrier semaphores. Data moves between devices by JAX's collectives and lax.ppermute only.
A program may use at most 64 MiB of HBM per device.

v0:
```python
import jax
import jax.numpy as jnp
from jax import lax
from jax.sharding import PartitionSpec as P

STEPS = 2


def shifted(value, axis, steps):
    count = lax.axis_size(axis)
    initial, last = (max(0, -steps), min(count, count - steps))
    return lax.ppermute(value, axis, [(source, source + steps) for source in range(initial, last)])


def padded_2(cells, sides, width):
    for axis, dim in sides:
        count = lax.axis_size(axis)
        ends = count - 1
        head = lax.slice_in_dim(cells, 0, width, axis=dim)
        tail = lax.slice_in_dim(cells, cells.shape[dim] - width, cells.shape[dim], axis=dim)
        cells = jnp.concatenate(
            [
                lax.ppermute(tail, axis, [(i, (i + 1) % count) for i in range(ends)]),
                cells,
                lax.ppermute(head, axis, [((i + 1) % count, i) for i in range(ends)]),
            ],
            axis=dim,
        )
    return cells


def interior(field):
    return field[1:-1]


def across(field):
    padded = jnp.pad(field, ((0, 0), (1, 1)))
    return padded[:, 2:] - padded[:, :-2]


def along(field):
    return field[2:] - field[:-2]


def advance(surface, east, north, depth_rows, rough_rows, wetness):
    depth_inner = interior(depth_rows)
    depth_safe = jnp.where(depth_inner > 0, depth_inner, 1.0)
    east_inner = interior(east)
    north_inner = interior(north)
    speed = jnp.sqrt(east_inner * east_inner + north_inner * north_inner + 1.0)
    rough_inner = interior(rough_rows)
    friction = 1.0 + 2.0 * rough_inner * rough_inner * speed / depth_safe ** (4.0 / 3.0)
    wet_inner = interior(wetness)
    new_east = wet_inner * (east_inner - 0.2 * depth_inner * across(interior(surface))) / friction
    new_north = wet_inner * (north_inner - 0.2 * depth_inner * along(surface)) / friction
    new_surface = interior(interior(surface)) - 0.25 * interior(wet_inner) * (
        interior(across(new_east)) + along(new_north)
    )
    return (new_surface, interior(new_east), interior(new_north))


def fold_rims(stacked, width):
    upper = stacked[:, :width]
    lower = stacked[:, stacked.shape[1] - width :]
    inner = stacked[:, width : stacked.shape[1] - width]
    from_below = shifted(upper, "tile", -1)
    from_above = shifted(lower, "tile", 1)
    inner = inner.at[:, inner.shape[1] - width :].add(from_below)
    return inner.at[:, :width].add(from_above)


def per_device(
    surface_start,
    east_start,
    north_start,
    still_depth,
    roughness,
    wet_masks,
    gauge_tiles,
    gauge_cells,
    gauge_values,
    survey_surface,
):
    row_count, col_count = still_depth.shape
    wet_float = wet_masks[0].astype(jnp.float32)
    statics = jnp.stack((still_depth, roughness))
    stored = []
    width = 2
    static_pad = padded_2(statics, (("tile", 1),), 2)
    surface, east, north = (surface_start[0], east_start[0], north_start[0])
    for step_index in range(STEPS):
        padded = padded_2(
            jnp.stack((surface, east, north, wet_float[step_index])), (("tile", 1),), 2
        )
        record = (padded[0], padded[1], padded[2], static_pad[0], static_pad[1], padded[3])
        stored.append(record)
        surface, east, north = advance(*record)
    strip_tiles = gauge_tiles[0, :, 0]
    tile_count = lax.axis_size("tile")
    listed = strip_tiles.shape[0]
    capacity = max(2, 2 * listed // tile_count)
    onehot = (strip_tiles[:, None] == jnp.arange(tile_count, dtype=jnp.int32)[None, :]).astype(
        jnp.int32
    )
    before = jnp.cumsum(onehot, axis=0) - onehot
    rank = jnp.sum(onehot * before, axis=1)
    slot = strip_tiles * capacity + rank
    cell_count = row_count * col_count
    send_cells = (
        jnp.full((tile_count * capacity,), cell_count, jnp.int32).at[slot].set(gauge_cells[0])
    )
    send_values = jnp.zeros((tile_count * capacity,), jnp.float32).at[slot].set(gauge_values[0])
    got_cells, got_values = (
        lax.all_to_all(
            send_cells.reshape(tile_count, capacity),
            "tile",
            split_axis=0,
            concat_axis=0,
            tiled=True,
        ),
        lax.all_to_all(
            send_values.reshape(tile_count, capacity),
            "tile",
            split_axis=0,
            concat_axis=0,
            tiled=True,
        ),
    )
    flat_cells = got_cells.reshape(-1)
    valid = flat_cells < cell_count
    seen = jnp.take(surface.reshape(-1), flat_cells, mode="fill", fill_value=0.0)
    missing = jnp.where(valid, seen - got_values.reshape(-1), 0.0)
    gauge_sense = (
        jnp.zeros((cell_count,), jnp.float32)
        .at[flat_cells]
        .add(missing, mode="drop")
        .reshape(row_count, col_count)
    )
    sense_surface = gauge_sense + (surface - survey_surface[0])
    sense_east = jnp.zeros_like(sense_surface)
    sense_north = jnp.zeros_like(sense_surface)
    rough_sense = jnp.zeros((row_count + 2 * width, col_count), jnp.float32)
    for step_index in reversed(range(STEPS)):
        surface_in, east_in, north_in, depth_rows, rough_rows, wetness = stored[step_index]

        def local_step(surface_arg, east_arg, north_arg, rough_arg):
            return advance(surface_arg, east_arg, north_arg, depth_rows, rough_arg, wetness)

        outputs, pullback = jax.vjp(local_step, surface_in, east_in, north_in, rough_rows)
        back_surface, back_east, back_north, back_rough = pullback(
            (sense_surface, sense_east, sense_north)
        )
        rough_sense = rough_sense + back_rough
        if step_index > 0:
            folded = fold_rims(jnp.stack((back_surface, back_east, back_north)), 2)
            sense_surface, sense_east, sense_north = (folded[0], folded[1], folded[2])
    local_grad = fold_rims(rough_sense[None], width)[0]
    total = lax.psum(local_grad, "event")
    share = col_count // lax.axis_size("event")
    return lax.dynamic_slice_in_dim(total, lax.axis_index("event") * share, share, 1)


def solution(mesh):
    placed = (
        P("event", "tile", None),
        P("event", "tile", None),
        P("event", "tile", None),
        P("tile", None),
        P("tile", None),
        P("event", None, "tile", None),
        P("event", "tile", None),
        P("event", "tile"),
        P("event", "tile"),
        P("event", "tile", None),
    )
    return jax.shard_map(
        per_device, mesh=mesh, in_specs=placed, out_specs=P("tile", "event"), check_vma=False
    )
```

profile of v0, /device:TPU:2, one launch (start us, length us, event | category | flops | bytes accessed | tf_op | source)
XLA Modules:
  0.0 217.5 jit_solution(9492636156233918174)
XLA Ops:
  6.5 1.4 pad_maximum_fusion.31
  7.9 3.8 %collective-permute-start = (f32[2,2,8192]{2,1,0:T(2,128)S(1)}, f32[2,2,8192]{2,1,0:T(2,128)S(1)}, u32[]{:S(2)}, u32[]{:S(2)}) collective-permute-start(f32[2,2,8192]{2,1,0:T(2,128)S(1)} %get-tuple-element.102), channel_id=1, source_target_pairs={{0,1},{1,2},{2,3},{3,4},{4,5},{5,6},{6,7},{7,8},{8,9},{9,10},{10,1... | collective-permute-start | bytes 393224 | tf_op jit(solution)/shard_map/ppermute | solution.py:23
  11.7 9.5 %collective-permute-start.1 = (f32[2,2,8192]{2,1,0:T(2,128)S(1)}, f32[2,2,8192]{2,1,0:T(2,128)}, u32[]{:S(2)}, u32[]{:S(2)}) collective-permute-start(f32[2,2,8192]{2,1,0:T(2,128)S(1)} %get-tuple-element.103), channel_id=1, source_target_pairs={{1,0},{2,1},{3,2},{4,3},{5,4},{6,5},{7,6},{8,7},{9,8},{10,9},{11,1... | collective-permute-start | bytes 393224 | tf_op jit(solution)/shard_map/ppermute | solution.py:25
  21.2 0.7 fusion.44
  21.9 0.6 reduce-window.6
  22.5 0.2 slice_reduce_fusion
  22.7 0.8 fusion.40
  23.5 0.7 compare_select_fusion.2
  24.2 1.6 scatter_custom_fusion
  25.8 0.7 all_to_all.12
  26.5 12.4 %all-to-all-start = ((s32[64,1,8]{2,1,0:T(1,128)}), s32[64,1,8]{2,1,0:T(1,128)S(1)}, u32[]{:S(2)}, u32[]{:S(2)}) async-start(s32[64,1,8]{2,1,0:T(1,128)} %bitcast.12), calls=%async_computation | async-start | bytes 65536 | tf_op jit(solution)/shard_map/all_to_all | solution.py:114
  38.9 1.1 convert_element_type.19
  40.0 1.6 scatter_custom_fusion.1
  41.6 0.7 all_to_all.14
  42.3 10.1 %all-to-all-done = s32[64,1,8]{2,1,0:T(1,128)S(1)} async-done(((s32[64,1,8]{2,1,0:T(1,128)}), s32[64,1,8]{2,1,0:T(1,128)S(1)}, u32[]{:S(2)}, u32[]{:S(2)}) %all-to-all-start) | async-done | bytes 2080 | tf_op jit(solution)/shard_map/all_to_all | solution.py:114
  52.4 5.5 %all-to-all-start.1 = ((f32[64,1,8]{2,1,0:T(1,128)}), f32[64,1,8]{2,1,0:T(1,128)S(1)}, u32[]{:S(2)}, u32[]{:S(2)}) async-start(f32[64,1,8]{2,1,0:T(1,128)} %bitcast.32), calls=%async_computation.1 | async-start | bytes 65536 | tf_op jit(solution)/shard_map/all_to_all | solution.py:121
  57.9 1.0 pad_maximum_fusion.27
  58.9 3.4 %collective-permute-start.2 = (f32[4,2,8192]{2,1,0:T(2,128)}, f32[4,2,8192]{2,1,0:T(2,128)S(1)}, u32[]{:S(2)}, u32[]{:S(2)}) collective-permute-start(f32[4,2,8192]{2,1,0:T(2,128)} %get-tuple-element.88), channel_id=1, source_target_pairs={{0,1},{1,2},{2,3},{3,4},{4,5},{5,6},{6,7},{7,8},{8,9},{9,10},{10,1... | collective-permute-start | bytes 786440 | tf_op jit(solution)/shard_map/ppermute | solution.py:23
  62.2 4.6 %collective-permute-start.3 = (f32[4,2,8192]{2,1,0:T(2,128)}, f32[4,2,8192]{2,1,0:T(2,128)S(1)}, u32[]{:S(2)}, u32[]{:S(2)}) collective-permute-start(f32[4,2,8192]{2,1,0:T(2,128)} %get-tuple-element.89), channel_id=1, source_target_pairs={{1,0},{2,1},{3,2},{4,3},{5,4},{6,5},{7,6},{8,7},{9,8},{10,9},{11,1... | collective-permute-start | bytes 786440 | tf_op jit(solution)/shard_map/ppermute | solution.py:25
  66.9 0.5 broadcast.320
  67.4 0.7 reduce.18
  68.3 3.0 %all-to-all-done.1 = f32[64,1,8]{2,1,0:T(1,128)S(1)} async-done(((f32[64,1,8]{2,1,0:T(1,128)}), f32[64,1,8]{2,1,0:T(1,128)S(1)}, u32[]{:S(2)}, u32[]{:S(2)}) %all-to-all-start.1) | async-done | bytes 2080 | tf_op jit(solution)/shard_map/all_to_all | solution.py:121
  71.4 0.5 broadcast.321
  71.9 0.7 reduce.19
  72.7 1.3 pad_maximum_fusion.3
  74.0 0.7 copy-done.18
  74.7 0.7 copy-done.20
  75.4 0.3 pad_maximum_fusion
  75.8 2.0 fusion.58
  77.9 1.4 pad_slice_fusion.3
  79.4 0.2 pad_maximum_fusion.23
  79.6 2.6 %collective-permute-start.4 = (f32[4,2,8192]{2,1,0:T(2,128)S(1)}, f32[4,2,8192]{2,1,0:T(2,128)S(1)}, u32[]{:S(2)}, u32[]{:S(2)}) collective-permute-start(f32[4,2,8192]{2,1,0:T(2,128)S(1)} %get-tuple-element.86), channel_id=1, source_target_pairs={{0,1},{1,2},{2,3},{3,4},{4,5},{5,6},{6,7},{7,8},{8,9},{9,10},{10,1... | collective-permute-start | bytes 786440 | tf_op jit(solution)/shard_map/ppermute | solution.py:23
  82.2 5.5 %collective-permute-start.5 = (f32[4,2,8192]{2,1,0:T(2,128)S(1)}, f32[4,2,8192]{2,1,0:T(2,128)S(1)}, u32[]{:S(2)}, u32[]{:S(2)}) collective-permute-start(f32[4,2,8192]{2,1,0:T(2,128)S(1)} %get-tuple-element.87), channel_id=1, source_target_pairs={{1,0},{2,1},{3,2},{4,3},{5,4},{6,5},{7,6},{8,7},{9,8},{10,9},{11,1... | collective-permute-start | bytes 786440 | tf_op jit(solution)/shard_map/ppermute | solution.py:25
  87.8 2.2 %collective-permute-done.4 = f32[4,2,8192]{2,1,0:T(2,128)S(1)} collective-permute-done((f32[4,2,8192]{2,1,0:T(2,128)S(1)}, f32[4,2,8192]{2,1,0:T(2,128)S(1)}, u32[]{:S(2)}, u32[]{:S(2)}) %collective-permute-start.4) | collective-permute-done | bytes 262176 | tf_op jit(solution)/shard_map/ppermute | solution.py:23
  90.0 1.5 collective-permute-done.5
  91.4 0.4 pad_maximum_fusion.1
  91.8 2.0 fusion.55
  93.9 0.3 pad_slice_fusion.1
  94.2 1.1 fusion.56
  95.3 0.8 fusion.29
  96.1 1.0 copy.16
  97.1 3.1 %gather_fusion = f32[512]{0:T(512)S(1)} fusion(f32[65536]{0:T(1024)S(1)} %bitcast.247, s32[1024]{0:T(1024)S(1)} %pad_clamp_fusion), kind=kCustom, calls=%fused_computation | custom fusion | bytes 6144 | tf_op jit(solution)/shard_map/jit(_take)/gather | solution.py:131
  100.3 3.9 %scatter_custom_fusion.2 = f32[65536]{0:T(1024)} fusion(s32[512]{0:T(512)S(1)} %bitcast.260, f32[512]{0:T(512)S(1)} %subtract_select_fusion, f32[]{:T(128)} %constant.144.clone.1), kind=kCustom, calls=%fused_computation.127 | custom fusion | flops 512 | bytes 262148 | tf_op jit(solution)/shard_map/scatter-add | solution.py:136
  104.2 1.0 reshape.257
  105.3 1.3 fusion.53
  106.7 0.2 copy-done.17
  106.8 1.7 fusion
  108.6 0.7 add_add_fusion.1
  109.5 0.3 pad_add_fusion.1
  109.8 0.2 fusion.12
  110.2 6.5 %collective-permute-start.6 = (f32[3,2,8192]{2,1,0:T(2,128)S(1)}, f32[3,2,8192]{2,1,0:T(2,128)S(1)}, u32[]{:S(2)}, u32[]{:S(2)}) collective-permute-start(f32[3,2,8192]{2,1,0:T(2,128)S(1)} %get-tuple-element.85), channel_id=1, source_target_pairs={{1,0},{2,1},{3,2},{4,3},{5,4},{6,5},{7,6},{8,7},{9,8},{10,9},{11,1... | collective-permute-start | bytes 589832 | tf_op jit(solution)/shard_map/ppermute | solution.py:12
  116.9 2.1 collective-permute-start.7
  119.0 0.9 collective-permute-done.6
  119.9 0.2 fusion.35
  120.1 6.6 %collective-permute-done.7 = f32[3,2,8192]{2,1,0:T(2,128)S(1)} collective-permute-done((f32[3,2,8192]{2,1,0:T(2,128)S(1)}, f32[3,2,8192]{2,1,0:T(2,128)S(1)}, u32[]{:S(2)}, u32[]{:S(2)}) %collective-permute-start.7) | collective-permute-done | bytes 196640 | tf_op jit(solution)/shard_map/ppermute | solution.py:12
  126.7 0.2 fusion.34
  127.1 1.5 fusion.1
  128.9 1.9 collective-permute-start.8
  130.8 3.9 %collective-permute-start.9 = (f32[1,2,8192]{2,1,0:T(2,128)S(1)}, f32[1,2,8192]{2,1,0:T(2,128)S(1)}, u32[]{:S(2)}, u32[]{:S(2)}) collective-permute-start(f32[1,2,8192]{2,1,0:T(2,128)S(1)} %get-tuple-element.92), channel_id=1, source_target_pairs={{0,1},{1,2},{2,3},{3,4},{4,5},{5,6},{6,7},{7,8},{8,9},{9,10},{10,1... | collective-permute-start | bytes 196616 | tf_op jit(solution)/shard_map/ppermute | solution.py:12
  134.8 0.3 collective-permute-done.8
  135.1 4.0 %collective-permute-done.9 = f32[1,2,8192]{2,1,0:T(2,128)S(1)} collective-permute-done((f32[1,2,8192]{2,1,0:T(2,128)S(1)}, f32[1,2,8192]{2,1,0:T(2,128)S(1)}, u32[]{:S(2)}, u32[]{:S(2)}) %collective-permute-start.9) | collective-permute-done | bytes 65568 | tf_op jit(solution)/shard_map/ppermute | solution.py:12
  139.2 0.7 copy-done.22
  139.9 69.4 %all-reduce.30.cloned.1.call-done = f32[8,8192]{1,0:T(8,128)} async-done(((f32[8,8192]{1,0:T(8,128)}), f32[8,8192]{1,0:T(8,128)}) %all-reduce.30.cloned.1.call-update) | async-done | bytes 262160 | tf_op jit(solution)/shard_map/psum | solution.py:158
  209.3 1.4 constant_dynamic-slice_fusion
  (79 shorter events, 2.0 us)
Async XLA Ops:
  6.5 51.3 %copy-start.9 = (f32[1,8,8192]{2,1,0:T(8,128)S(1)}, f32[1,8,8192]{2,1,0:T(8,128)}, u32[]{:S(2)}) copy-start(f32[1,8,8192]{2,1,0:T(8,128)} %param.18) | copy-start | bytes 786436
  6.5 51.3 %copy-start.12 = (f32[1,8,8192]{2,1,0:T(8,128)S(1)}, f32[1,8,8192]{2,1,0:T(8,128)}, u32[]{:S(2)}) copy-start(f32[1,8,8192]{2,1,0:T(8,128)} %param.19) | copy-start | bytes 786436
  6.5 51.4 %copy-start.10 = (f32[1,8,8192]{2,1,0:T(8,128)S(1)}, f32[1,8,8192]{2,1,0:T(8,128)}, u32[]{:S(2)}) copy-start(f32[1,8,8192]{2,1,0:T(8,128)} %param.20) | copy-start | bytes 786436
  7.9 64.8 %collective-permute-start = (f32[2,2,8192]{2,1,0:T(2,128)S(1)}, f32[2,2,8192]{2,1,0:T(2,128)S(1)}, u32[]{:S(2)}, u32[]{:S(2)}) collective-permute-start(f32[2,2,8192]{2,1,0:T(2,128)S(1)} %get-tuple-element.102), channel_id=1, source_target_pairs={{0,1},{1,2},{2,3},{3,4},{4,5},{5,6},{6,7},{7,8},{8,9},{9,10},{10,1... | collective-permute-start | bytes 393224 | tf_op jit(solution)/shard_map/ppermute | solution.py:23
  11.7 61.0 %collective-permute-start.1 = (f32[2,2,8192]{2,1,0:T(2,128)S(1)}, f32[2,2,8192]{2,1,0:T(2,128)}, u32[]{:S(2)}, u32[]{:S(2)}) collective-permute-start(f32[2,2,8192]{2,1,0:T(2,128)S(1)} %get-tuple-element.103), channel_id=1, source_target_pairs={{1,0},{2,1},{3,2},{4,3},{5,4},{6,5},{7,6},{8,7},{9,8},{10,9},{11,1... | collective-permute-start | bytes 393224 | tf_op jit(solution)/shard_map/ppermute | solution.py:25
  26.5 25.9 %all-to-all-start = ((s32[64,1,8]{2,1,0:T(1,128)}), s32[64,1,8]{2,1,0:T(1,128)S(1)}, u32[]{:S(2)}, u32[]{:S(2)}) async-start(s32[64,1,8]{2,1,0:T(1,128)} %bitcast.12), calls=%async_computation | async-start | bytes 65536 | tf_op jit(solution)/shard_map/all_to_all | solution.py:114
  40.0 39.3 %copy-start.2 = (f32[1,2,8,8192]{3,2,1,0:T(8,128)}, f32[1,2,8,8192]{3,2,1,0:T(8,128)S(1)}, u32[]{:S(2)}) copy-start(f32[1,2,8,8192]{3,2,1,0:T(8,128)S(1)} %convert_element_type.19) | copy-start | bytes 1572868
  52.4 19.0 %all-to-all-start.1 = ((f32[64,1,8]{2,1,0:T(1,128)}), f32[64,1,8]{2,1,0:T(1,128)S(1)}, u32[]{:S(2)}, u32[]{:S(2)}) async-start(f32[64,1,8]{2,1,0:T(1,128)} %bitcast.32), calls=%async_computation.1 | async-start | bytes 65536 | tf_op jit(solution)/shard_map/all_to_all | solution.py:121
  57.8 151.5 %all-reduce.30.cloned.1.call-start = ((), (), s32[]{:S(2)}) async-start(), calls=%async_computation.2 | async-start | bytes 524288 | tf_op jit(solution)/shard_map/psum | solution.py:158
  58.9 15.1 %collective-permute-start.2 = (f32[4,2,8192]{2,1,0:T(2,128)}, f32[4,2,8192]{2,1,0:T(2,128)S(1)}, u32[]{:S(2)}, u32[]{:S(2)}) collective-permute-start(f32[4,2,8192]{2,1,0:T(2,128)} %get-tuple-element.88), channel_id=1, source_target_pairs={{0,1},{1,2},{2,3},{3,4},{4,5},{5,6},{6,7},{7,8},{8,9},{9,10},{10,1... | collective-permute-start | bytes 786440 | tf_op jit(solution)/shard_map/ppermute | solution.py:23
  62.2 11.8 %collective-permute-start.3 = (f32[4,2,8192]{2,1,0:T(2,128)}, f32[4,2,8192]{2,1,0:T(2,128)S(1)}, u32[]{:S(2)}, u32[]{:S(2)}) collective-permute-start(f32[4,2,8192]{2,1,0:T(2,128)} %get-tuple-element.89), channel_id=1, source_target_pairs={{1,0},{2,1},{3,2},{4,3},{5,4},{6,5},{7,6},{8,7},{9,8},{10,9},{11,1... | collective-permute-start | bytes 786440 | tf_op jit(solution)/shard_map/ppermute | solution.py:25
  74.0 0.7 copy-start.18
  74.7 0.7 copy-start.20
  75.7 2.1 copy-start
  75.8 2.1 copy-start.11
  75.8 2.1 copy-start.13
  75.8 2.1 copy-start.19
  75.8 2.1 copy-start.21
  77.8 1.5 copy-start.7
  79.6 10.4 %collective-permute-start.4 = (f32[4,2,8192]{2,1,0:T(2,128)S(1)}, f32[4,2,8192]{2,1,0:T(2,128)S(1)}, u32[]{:S(2)}, u32[]{:S(2)}) collective-permute-start(f32[4,2,8192]{2,1,0:T(2,128)S(1)} %get-tuple-element.86), channel_id=1, source_target_pairs={{0,1},{1,2},{2,3},{3,4},{4,5},{5,6},{6,7},{7,8},{8,9},{9,10},{10,1... | collective-permute-start | bytes 786440 | tf_op jit(solution)/shard_map/ppermute | solution.py:23
  82.2 9.2 %collective-permute-start.5 = (f32[4,2,8192]{2,1,0:T(2,128)S(1)}, f32[4,2,8192]{2,1,0:T(2,128)S(1)}, u32[]{:S(2)}, u32[]{:S(2)}) collective-permute-start(f32[4,2,8192]{2,1,0:T(2,128)S(1)} %get-tuple-element.87), channel_id=1, source_target_pairs={{1,0},{2,1},{3,2},{4,3},{5,4},{6,5},{7,6},{8,7},{9,8},{10,9},{11,1... | collective-permute-start | bytes 786440 | tf_op jit(solution)/shard_map/ppermute | solution.py:25
  93.9 1.4 copy-start.5
  94.2 1.1 copy-start.3
  105.2 1.4 copy-start.6
  105.2 1.4 copy-start.16
  105.3 1.6 copy-start.17
  110.2 9.7 %collective-permute-start.6 = (f32[3,2,8192]{2,1,0:T(2,128)S(1)}, f32[3,2,8192]{2,1,0:T(2,128)S(1)}, u32[]{:S(2)}, u32[]{:S(2)}) collective-permute-start(f32[3,2,8192]{2,1,0:T(2,128)S(1)} %get-tuple-element.85), channel_id=1, source_target_pairs={{1,0},{2,1},{3,2},{4,3},{5,4},{6,5},{7,6},{8,7},{9,8},{10,9},{11,1... | collective-permute-start | bytes 589832 | tf_op jit(solution)/shard_map/ppermute | solution.py:12
  116.8 10.1 %copy-start.4 = (f32[1,2,8,8192]{3,2,1,0:T(8,128)S(1)}, f32[1,2,8,8192]{3,2,1,0:T(8,128)}, u32[]{:S(2)}) copy-start(f32[1,2,8,8192]{3,2,1,0:T(8,128)} %copy-done.2) | copy-start | bytes 1572868
  116.9 9.8 %collective-permute-start.7 = (f32[3,2,8192]{2,1,0:T(2,128)S(1)}, f32[3,2,8192]{2,1,0:T(2,128)S(1)}, u32[]{:S(2)}, u32[]{:S(2)}) collective-permute-start(f32[3,2,8192]{2,1,0:T(2,128)S(1)} %get-tuple-element.84), channel_id=1, source_target_pairs={{0,1},{1,2},{2,3},{3,4},{4,5},{5,6},{6,7},{7,8},{8,9},{9,10},{10,1... | collective-permute-start | bytes 589832 | tf_op jit(solution)/shard_map/ppermute | solution.py:12
  120.1 7.0 %copy-start.1 = (f32[4,12,8192]{2,1,0:T(8,128)S(1)}, f32[4,12,8192]{2,1,0:T(8,128)}, u32[]{:S(2)}) copy-start(f32[4,12,8192]{2,1,0:T(8,128)} %copy-done) | copy-start | bytes 4718596
  120.1 7.0 %copy-start.8 = (f32[10,8192]{1,0:T(8,128)S(1)}, f32[10,8192]{1,0:T(8,128)}, u32[]{:S(2)}) copy-start(f32[10,8192]{1,0:T(8,128)} %copy-done.7) | copy-start | bytes 983044
  120.1 7.0 %copy-start.14 = (f32[10,8192]{1,0:T(8,128)S(1)}, f32[10,8192]{1,0:T(8,128)}, u32[]{:S(2)}) copy-start(f32[10,8192]{1,0:T(8,128)} %get-tuple-element.75) | copy-start | bytes 983044
  120.1 7.0 %copy-start.15 = (f32[10,8192]{1,0:T(8,128)S(1)}, f32[10,8192]{1,0:T(8,128)}, u32[]{:S(2)}) copy-start(f32[10,8192]{1,0:T(8,128)} %get-tuple-element.109) | copy-start | bytes 983044
  128.9 6.2 %collective-permute-start.8 = (f32[1,2,8192]{2,1,0:T(2,128)S(1)}, f32[1,2,8192]{2,1,0:T(2,128)S(1)}, u32[]{:S(2)}, u32[]{:S(2)}) collective-permute-start(f32[1,2,8192]{2,1,0:T(2,128)S(1)} %get-tuple-element.93), channel_id=1, source_target_pairs={{1,0},{2,1},{3,2},{4,3},{5,4},{6,5},{7,6},{8,7},{9,8},{10,9},{11,1... | collective-permute-start | bytes 196616 | tf_op jit(solution)/shard_map/ppermute | solution.py:12
  130.8 8.3 %collective-permute-start.9 = (f32[1,2,8192]{2,1,0:T(2,128)S(1)}, f32[1,2,8192]{2,1,0:T(2,128)S(1)}, u32[]{:S(2)}, u32[]{:S(2)}) collective-permute-start(f32[1,2,8192]{2,1,0:T(2,128)S(1)} %get-tuple-element.92), channel_id=1, source_target_pairs={{0,1},{1,2},{2,3},{3,4},{4,5},{5,6},{6,7},{7,8},{8,9},{9,10},{10,1... | collective-permute-start | bytes 196616 | tf_op jit(solution)/shard_map/ppermute | solution.py:12
  139.1 0.7 copy-start.22
Sparse Core Ops, SparseCore 0:
  140.0 69.2 all-reduce.29
where the time goes:
time: 218 us
  waiting for transfers between devices  98 us (45%)
  starting transfers between devices  61.7 us (28%)
  other arithmetic  28.1 us (13%)
  local copies, waits for them, and re-layouts  15.7 us (7%)
  between operations  14.1 us (6%)
    psum x1, waiting for transfers between devices, per_device(): total = lax.psum(local_grad, 'event')  69.4 us
    ppermute x3, starting transfers between devices, padded_2(): lax.ppermute(head, axis, [((i + 1) % count, i) for i in range(ends)])  19.6 us
    ppermute x4, starting transfers between devices, shifted(): lax.ppermute(value, axis, [(source, source + steps) for source in range(i...  14.4 us
    all_to_all x1, starting transfers between devices, per_device(): lax.all_to_all(send_cells.reshape(tile_count, capacity), 'tile', split_ax...  12.4 us
    ppermute x4, waiting for transfers between devices, shifted(): lax.ppermute(value, axis, [(source, source + steps) for source in range(i...  11.8 us
    all_to_all x1, waiting for transfers between devices, per_device(): lax.all_to_all(send_cells.reshape(tile_count, capacity), 'tile', split_ax...  10.1 us
    ppermute x3, starting transfers between devices, padded_2(): lax.ppermute(tail, axis, [(i, (i + 1) % count) for i in range(ends)])  9.78 us
    all_to_all x1, starting transfers between devices, per_device(): lax.all_to_all(send_values.reshape(tile_count, capacity), 'tile', split_a...  5.45 us
  transfers between devices with their start and end apart: 13, of which 9 were waited for; matrix products, arithmetic and copies ran while one was open for 6% of the time, Pallas kernels for 0%

commit v1 on v0

--- a/solution.py
+++ b/solution.py
@@ -155,7 +155,10 @@
             folded = fold_rims(jnp.stack((back_surface, back_east, back_north)), 2)
             sense_surface, sense_east, sense_north = (folded[0], folded[1], folded[2])
     local_grad = fold_rims(rough_sense[None], width)[0]
-    total = lax.psum(local_grad, "event")
+    count_2, total = (lax.axis_size("event"), local_grad)
+    for far in [1 << k for k in range(count_2.bit_length() - 1)]:
+        pairs = [(i_2, i_2 ^ far) for i_2 in range(count_2)]
+        total = total + lax.ppermute(total, "event", pairs)
     share = col_count // lax.axis_size("event")
     return lax.dynamic_slice_in_dim(total, lax.axis_index("event") * share, share, 1)
 

time: 218 us -> 159 us (0.73)
  the two profiles are of different devices: /device:TPU:2 before, /device:TPU:18 now
where the time goes in v1:
time: 159 us; the launch traced here: 158 us
  starting transfers between devices  69 us (43%)
  waiting for transfers between devices  45.8 us (29%)
  other arithmetic  28.8 us (18%)
  local copies, waits for them, and re-layouts  13.6 us (9%)
    ppermute x3, starting transfers between devices, padded_2(): lax.ppermute(head, axis, [((i + 1) % count, i) for i in range(ends)])  19.7 us
    ppermute x3, waiting for transfers between devices, per_device(): total = total + lax.ppermute(total, 'event', pairs)  17.2 us
    ppermute x4, starting transfers between devices, shifted(): lax.ppermute(value, axis, [(source, source + steps) for source in range(i...  14.4 us
    all_to_all x1, starting transfers between devices, per_device(): lax.all_to_all(send_cells.reshape(tile_count, capacity), 'tile', split_ax...  12.4 us
    ppermute x4, waiting for transfers between devices, shifted(): lax.ppermute(value, axis, [(source, source + steps) for source in range(i...  11.8 us
    all_to_all x1, waiting for transfers between devices, per_device(): lax.all_to_all(send_cells.reshape(tile_count, capacity), 'tile', split_ax...  10.1 us
    ppermute x3, starting transfers between devices, padded_2(): lax.ppermute(tail, axis, [(i, (i + 1) % count) for i in range(ends)])  9.69 us
    ppermute x3, starting transfers between devices, per_device(): total = total + lax.ppermute(total, 'event', pairs)  7.36 us
  transfers between devices with their start and end apart: 15, of which 11 were waited for; matrix products, arithmetic and copies ran while one was open for 8% of the time, Pallas kernels for 0%

profile of v1, /device:TPU:18, one launch (start us, length us, event | category | flops | bytes accessed | tf_op | source)
XLA Modules:
  0.0 158.0 jit_solution(10710406579113047772)
XLA Ops:
  0.0 1.4 pad_maximum_fusion.31
  1.4 3.8 %collective-permute-start = (f32[2,2,8192]{2,1,0:T(2,128)S(1)}, f32[2,2,8192]{2,1,0:T(2,128)S(1)}, u32[]{:S(2)}, u32[]{:S(2)}) collective-permute-start(f32[2,2,8192]{2,1,0:T(2,128)S(1)} %get-tuple-element.102), channel_id=1, source_target_pairs={{0,1},{1,2},{2,3},{3,4},{4,5},{5,6},{6,7},{7,8},{8,9},{9,10},{10,1... | collective-permute-start | bytes 393224 | tf_op jit(solution)/shard_map/ppermute | solution.py:23
  5.2 9.5 %collective-permute-start.1 = (f32[2,2,8192]{2,1,0:T(2,128)S(1)}, f32[2,2,8192]{2,1,0:T(2,128)}, u32[]{:S(2)}, u32[]{:S(2)}) collective-permute-start(f32[2,2,8192]{2,1,0:T(2,128)S(1)} %get-tuple-element.103), channel_id=1, source_target_pairs={{1,0},{2,1},{3,2},{4,3},{5,4},{6,5},{7,6},{8,7},{9,8},{10,9},{11,1... | collective-permute-start | bytes 393224 | tf_op jit(solution)/shard_map/ppermute | solution.py:25
  14.7 0.7 fusion.44
  15.4 0.6 reduce-window.6
  16.0 0.2 slice_reduce_fusion
  16.2 0.8 fusion.40
  17.0 0.7 compare_select_fusion.2
  17.7 1.6 scatter_custom_fusion
  19.2 0.7 all_to_all.12
  19.9 12.4 %all-to-all-start = ((s32[64,1,8]{2,1,0:T(1,128)}), s32[64,1,8]{2,1,0:T(1,128)S(1)}, u32[]{:S(2)}, u32[]{:S(2)}) async-start(s32[64,1,8]{2,1,0:T(1,128)} %bitcast.12), calls=%async_computation | async-start | bytes 65536 | tf_op jit(solution)/shard_map/all_to_all | solution.py:114
  32.4 1.1 convert_element_type.19
  33.5 1.6 scatter_custom_fusion.1
  35.0 0.7 all_to_all.14
  35.7 10.1 %all-to-all-done = s32[64,1,8]{2,1,0:T(1,128)S(1)} async-done(((s32[64,1,8]{2,1,0:T(1,128)}), s32[64,1,8]{2,1,0:T(1,128)S(1)}, u32[]{:S(2)}, u32[]{:S(2)}) %all-to-all-start) | async-done | bytes 2080 | tf_op jit(solution)/shard_map/all_to_all | solution.py:114
  45.8 5.5 %all-to-all-start.1 = ((f32[64,1,8]{2,1,0:T(1,128)}), f32[64,1,8]{2,1,0:T(1,128)S(1)}, u32[]{:S(2)}, u32[]{:S(2)}) async-start(f32[64,1,8]{2,1,0:T(1,128)} %bitcast.32), calls=%async_computation.1 | async-start | bytes 65536 | tf_op jit(solution)/shard_map/all_to_all | solution.py:121
  51.4 1.0 pad_maximum_fusion.27
  52.3 3.4 %collective-permute-start.2 = (f32[4,2,8192]{2,1,0:T(2,128)}, f32[4,2,8192]{2,1,0:T(2,128)S(1)}, u32[]{:S(2)}, u32[]{:S(2)}) collective-permute-start(f32[4,2,8192]{2,1,0:T(2,128)} %get-tuple-element.88), channel_id=1, source_target_pairs={{0,1},{1,2},{2,3},{3,4},{4,5},{5,6},{6,7},{7,8},{8,9},{9,10},{10,1... | collective-permute-start | bytes 786440 | tf_op jit(solution)/shard_map/ppermute | solution.py:23
  55.7 4.6 %collective-permute-start.3 = (f32[4,2,8192]{2,1,0:T(2,128)}, f32[4,2,8192]{2,1,0:T(2,128)S(1)}, u32[]{:S(2)}, u32[]{:S(2)}) collective-permute-start(f32[4,2,8192]{2,1,0:T(2,128)} %get-tuple-element.89), channel_id=1, source_target_pairs={{1,0},{2,1},{3,2},{4,3},{5,4},{6,5},{7,6},{8,7},{9,8},{10,9},{11,1... | collective-permute-start | bytes 786440 | tf_op jit(solution)/shard_map/ppermute | solution.py:25
  60.4 0.5 broadcast.320
  60.9 0.7 reduce.18
  61.8 3.1 %all-to-all-done.1 = f32[64,1,8]{2,1,0:T(1,128)S(1)} async-done(((f32[64,1,8]{2,1,0:T(1,128)}), f32[64,1,8]{2,1,0:T(1,128)S(1)}, u32[]{:S(2)}, u32[]{:S(2)}) %all-to-all-start.1) | async-done | bytes 2080 | tf_op jit(solution)/shard_map/all_to_all | solution.py:121
  64.9 0.5 broadcast.321
  65.4 0.7 reduce.19
  66.3 1.3 pad_maximum_fusion.3
  67.6 0.7 copy-done.18
  68.3 0.7 copy-done.20
  69.0 0.3 pad_maximum_fusion
  69.4 2.0 %fusion.58 = (f32[10,8192]{1,0:T(8,128)S(1)}, f32[10,8192]{1,0:T(8,128)S(1)}, f32[10,8192]{1,0:T(8,128)}) fusion(f32[2,12,8192]{2,1,0:T(8,128)S(1)} %pad_maximum_fusion.3, f32[4,12,8192]{2,1,0:T(8,128)S(1)} %pad_maximum_fusion, f32[10,8192]{1,0:T(8,128)S(1)} %slice_bitcast_fusion.5), kind=kLoop, calls=%fused_computation.162 | loop fusion | flops 1392640 | bytes 2949120 | tf_op jit(solution)/shard_map/div | solution.py:54
  71.5 1.4 pad_slice_fusion.3
  73.2 2.5 %collective-permute-start.4 = (f32[4,2,8192]{2,1,0:T(2,128)S(1)}, f32[4,2,8192]{2,1,0:T(2,128)S(1)}, u32[]{:S(2)}, u32[]{:S(2)}) collective-permute-start(f32[4,2,8192]{2,1,0:T(2,128)S(1)} %get-tuple-element.86), channel_id=1, source_target_pairs={{0,1},{1,2},{2,3},{3,4},{4,5},{5,6},{6,7},{7,8},{8,9},{9,10},{10,1... | collective-permute-start | bytes 786440 | tf_op jit(solution)/shard_map/ppermute | solution.py:23
  75.7 5.6 %collective-permute-start.5 = (f32[4,2,8192]{2,1,0:T(2,128)S(1)}, f32[4,2,8192]{2,1,0:T(2,128)S(1)}, u32[]{:S(2)}, u32[]{:S(2)}) collective-permute-start(f32[4,2,8192]{2,1,0:T(2,128)S(1)} %get-tuple-element.87), channel_id=1, source_target_pairs={{1,0},{2,1},{3,2},{4,3},{5,4},{6,5},{7,6},{8,7},{9,8},{10,9},{11,1... | collective-permute-start | bytes 786440 | tf_op jit(solution)/shard_map/ppermute | solution.py:25
  81.4 2.2 %collective-permute-done.4 = f32[4,2,8192]{2,1,0:T(2,128)S(1)} collective-permute-done((f32[4,2,8192]{2,1,0:T(2,128)S(1)}, f32[4,2,8192]{2,1,0:T(2,128)S(1)}, u32[]{:S(2)}, u32[]{:S(2)}) %collective-permute-start.4) | collective-permute-done | bytes 262176 | tf_op jit(solution)/shard_map/ppermute | solution.py:23
  83.6 1.5 collective-permute-done.5
  85.0 0.4 pad_maximum_fusion.1
  85.4 2.0 %fusion.55 = (f32[10,8192]{1,0:T(8,128)S(1)}, f32[10,8192]{1,0:T(8,128)}, f32[10,8192]{1,0:T(8,128)S(1)}) fusion(f32[10,8192]{1,0:T(8,128)S(1)} %slice_bitcast_fusion.1, f32[2,12,8192]{2,1,0:T(8,128)S(1)} %pad_maximum_fusion.3, f32[4,12,8192]{2,1,0:T(8,128)S(1)} %pad_maximum_fusion.1), kind=kLoop, calls=%fused_computation.160 | loop fusion | flops 1392640 | bytes 2949120 | tf_op jit(solution)/shard_map/div | solution.py:54
  87.4 0.3 pad_slice_fusion.1
  87.8 1.1 fusion.56
  88.9 0.8 fusion.29
  89.7 1.0 copy.16
  90.7 3.1 %gather_fusion = f32[512]{0:T(512)S(1)} fusion(f32[65536]{0:T(1024)S(1)} %bitcast.247, s32[1024]{0:T(1024)S(1)} %pad_clamp_fusion), kind=kCustom, calls=%fused_computation | custom fusion | bytes 6144 | tf_op jit(solution)/shard_map/jit(_take)/gather | solution.py:131
  93.9 3.9 %scatter_custom_fusion.2 = f32[65536]{0:T(1024)} fusion(s32[512]{0:T(512)S(1)} %bitcast.260, f32[512]{0:T(512)S(1)} %subtract_select_fusion, f32[]{:T(128)} %constant.144.clone.1), kind=kCustom, calls=%fused_computation.127 | custom fusion | flops 512 | bytes 262148 | tf_op jit(solution)/shard_map/scatter-add | solution.py:136
  97.8 1.0 reshape.257
  98.9 1.3 fusion.53
  100.4 1.7 %fusion = (f32[10,8192]{1,0:T(8,128)S(1)}, f32[10,8192]{1,0:T(8,128)S(1)}, f32[10,8192]{1,0:T(8,128)S(1)}, f32[10,8192]{1,0:T(8,128)S(1)}, f32[10,8192]{1,0:T(8,128)S(1)}) fusion(f32[2,12,8192]{2,1,0:T(8,128)S(1)} %pad_maximum_fusion.3, f32[4,12,8192]{2,1,0:T(8,128)S(1)} %pad_maximum_fusion.1, f32[10,8192]{1,0:T(8,128)S(1)} %copy-done.16, ...), kind=kLoop, calls=%fused_computation.14 | loop fusion | flops 2621440 | bytes 5439528 | tf_op jit(solution)/shard_map/transpose(jvp())/add_any | solution.py:52
  102.2 0.7 add_add_fusion.1
  103.1 0.3 pad_add_fusion.1
  103.8 6.5 %collective-permute-start.6 = (f32[3,2,8192]{2,1,0:T(2,128)S(1)}, f32[3,2,8192]{2,1,0:T(2,128)S(1)}, u32[]{:S(2)}, u32[]{:S(2)}) collective-permute-start(f32[3,2,8192]{2,1,0:T(2,128)S(1)} %get-tuple-element.85), channel_id=1, source_target_pairs={{1,0},{2,1},{3,2},{4,3},{5,4},{6,5},{7,6},{8,7},{9,8},{10,9},{11,1... | collective-permute-start | bytes 589832 | tf_op jit(solution)/shard_map/ppermute | solution.py:12
  110.5 2.1 %collective-permute-start.7 = (f32[3,2,8192]{2,1,0:T(2,128)S(1)}, f32[3,2,8192]{2,1,0:T(2,128)S(1)}, u32[]{:S(2)}, u32[]{:S(2)}) collective-permute-start(f32[3,2,8192]{2,1,0:T(2,128)S(1)} %get-tuple-element.84), channel_id=1, source_target_pairs={{0,1},{1,2},{2,3},{3,4},{4,5},{5,6},{6,7},{7,8},{8,9},{9,10},{10,1... | collective-permute-start | bytes 589832 | tf_op jit(solution)/shard_map/ppermute | solution.py:12
  112.6 0.9 collective-permute-done.6
  113.5 0.2 fusion.35
  113.7 6.6 %collective-permute-done.7 = f32[3,2,8192]{2,1,0:T(2,128)S(1)} collective-permute-done((f32[3,2,8192]{2,1,0:T(2,128)S(1)}, f32[3,2,8192]{2,1,0:T(2,128)S(1)}, u32[]{:S(2)}, u32[]{:S(2)}) %collective-permute-start.7) | collective-permute-done | bytes 196640 | tf_op jit(solution)/shard_map/ppermute | solution.py:12
  120.7 1.5 fusion.1
  122.4 1.9 %collective-permute-start.8 = (f32[1,2,8192]{2,1,0:T(2,128)S(1)}, f32[1,2,8192]{2,1,0:T(2,128)S(1)}, u32[]{:S(2)}, u32[]{:S(2)}) collective-permute-start(f32[1,2,8192]{2,1,0:T(2,128)S(1)} %get-tuple-element.93), channel_id=1, source_target_pairs={{1,0},{2,1},{3,2},{4,3},{5,4},{6,5},{7,6},{8,7},{9,8},{10,9},{11,1... | collective-permute-start | bytes 196616 | tf_op jit(solution)/shard_map/ppermute | solution.py:12
  124.4 3.9 %collective-permute-start.9 = (f32[1,2,8192]{2,1,0:T(2,128)S(1)}, f32[1,2,8192]{2,1,0:T(2,128)S(1)}, u32[]{:S(2)}, u32[]{:S(2)}) collective-permute-start(f32[1,2,8192]{2,1,0:T(2,128)S(1)} %get-tuple-element.92), channel_id=1, source_target_pairs={{0,1},{1,2},{2,3},{3,4},{4,5},{5,6},{6,7},{7,8},{8,9},{9,10},{10,1... | collective-permute-start | bytes 196616 | tf_op jit(solution)/shard_map/ppermute | solution.py:12
  128.3 0.3 collective-permute-done.8
  128.7 4.0 %collective-permute-done.9 = f32[1,2,8192]{2,1,0:T(2,128)S(1)} collective-permute-done((f32[1,2,8192]{2,1,0:T(2,128)S(1)}, f32[1,2,8192]{2,1,0:T(2,128)S(1)}, u32[]{:S(2)}, u32[]{:S(2)}) %collective-permute-start.9) | collective-permute-done | bytes 65568 | tf_op jit(solution)/shard_map/ppermute | solution.py:12
  132.7 1.9 %collective-permute-start.10 = (f32[8,8192]{1,0:T(8,128)S(1)}, f32[8,8192]{1,0:T(8,128)S(1)}, u32[]{:S(2)}, u32[]{:S(2)}) collective-permute-start(f32[8,8192]{1,0:T(8,128)S(1)} %fusion.42), channel_id=1, source_target_pairs={{0,64},{64,0},{128,192},{192,128},{256,320},{320,256},{384,448},{4... | collective-permute-start | bytes 786440 | tf_op jit(solution)/shard_map/ppermute | solution.py:161
  134.7 1.5 collective-permute-done.10
  136.2 3.2 %collective-permute-start.11 = (f32[8,8192]{1,0:T(8,128)S(1)}, f32[8,8192]{1,0:T(8,128)S(1)}, u32[]{:S(2)}, u32[]{:S(2)}) collective-permute-start(f32[8,8192]{1,0:T(8,128)S(1)} %add.191), channel_id=1, source_target_pairs={{0,128},{64,192},{128,0},{192,64},{256,384},{320,448},{384,256},{4... | collective-permute-start | bytes 786440 | tf_op jit(solution)/shard_map/ppermute | solution.py:161
  139.4 7.0 %collective-permute-done.11 = f32[8,8192]{1,0:T(8,128)S(1)} collective-permute-done((f32[8,8192]{1,0:T(8,128)S(1)}, f32[8,8192]{1,0:T(8,128)S(1)}, u32[]{:S(2)}, u32[]{:S(2)}) %collective-permute-start.11) | collective-permute-done | bytes 262176 | tf_op jit(solution)/shard_map/ppermute | solution.py:161
  146.5 2.2 %collective-permute-start.12 = (f32[8,8192]{1,0:T(8,128)S(1)}, f32[8,8192]{1,0:T(8,128)S(1)}, u32[]{:S(2)}, u32[]{:S(2)}) collective-permute-start(f32[8,8192]{1,0:T(8,128)S(1)} %add.192), channel_id=1, source_target_pairs={{0,256},{64,320},{128,384},{192,448},{256,0},{320,64},{384,128},{4... | collective-permute-start | bytes 786440 | tf_op jit(solution)/shard_map/ppermute | solution.py:161
  148.7 8.6 %collective-permute-done.12 = f32[8,8192]{1,0:T(8,128)S(1)} collective-permute-done((f32[8,8192]{1,0:T(8,128)S(1)}, f32[8,8192]{1,0:T(8,128)S(1)}, u32[]{:S(2)}, u32[]{:S(2)}) %collective-permute-start.12) | collective-permute-done | bytes 262176 | tf_op jit(solution)/shard_map/ppermute | solution.py:161
  157.4 0.6 dynamic-slice_add_fusion
  (82 shorter events, 2.7 us)
Async XLA Ops:
  0.0 51.3 %copy-start.9 = (f32[1,8,8192]{2,1,0:T(8,128)S(1)}, f32[1,8,8192]{2,1,0:T(8,128)}, u32[]{:S(2)}) copy-start(f32[1,8,8192]{2,1,0:T(8,128)} %param.18) | copy-start | bytes 786436
  0.0 51.3 %copy-start.12 = (f32[1,8,8192]{2,1,0:T(8,128)S(1)}, f32[1,8,8192]{2,1,0:T(8,128)}, u32[]{:S(2)}) copy-start(f32[1,8,8192]{2,1,0:T(8,128)} %param.19) | copy-start | bytes 786436
  0.0 51.3 %copy-start.10 = (f32[1,8,8192]{2,1,0:T(8,128)S(1)}, f32[1,8,8192]{2,1,0:T(8,128)}, u32[]{:S(2)}) copy-start(f32[1,8,8192]{2,1,0:T(8,128)} %param.20) | copy-start | bytes 786436
  1.4 64.9 %collective-permute-start = (f32[2,2,8192]{2,1,0:T(2,128)S(1)}, f32[2,2,8192]{2,1,0:T(2,128)S(1)}, u32[]{:S(2)}, u32[]{:S(2)}) collective-permute-start(f32[2,2,8192]{2,1,0:T(2,128)S(1)} %get-tuple-element.102), channel_id=1, source_target_pairs={{0,1},{1,2},{2,3},{3,4},{4,5},{5,6},{6,7},{7,8},{8,9},{9,10},{10,1... | collective-permute-start | bytes 393224 | tf_op jit(solution)/shard_map/ppermute | solution.py:23
  5.2 61.1 %collective-permute-start.1 = (f32[2,2,8192]{2,1,0:T(2,128)S(1)}, f32[2,2,8192]{2,1,0:T(2,128)}, u32[]{:S(2)}, u32[]{:S(2)}) collective-permute-start(f32[2,2,8192]{2,1,0:T(2,128)S(1)} %get-tuple-element.103), channel_id=1, source_target_pairs={{1,0},{2,1},{3,2},{4,3},{5,4},{6,5},{7,6},{8,7},{9,8},{10,9},{11,1... | collective-permute-start | bytes 393224 | tf_op jit(solution)/shard_map/ppermute | solution.py:25
  19.9 25.9 %all-to-all-start = ((s32[64,1,8]{2,1,0:T(1,128)}), s32[64,1,8]{2,1,0:T(1,128)S(1)}, u32[]{:S(2)}, u32[]{:S(2)}) async-start(s32[64,1,8]{2,1,0:T(1,128)} %bitcast.12), calls=%async_computation | async-start | bytes 65536 | tf_op jit(solution)/shard_map/all_to_all | solution.py:114
  33.4 39.4 %copy-start.2 = (f32[1,2,8,8192]{3,2,1,0:T(8,128)}, f32[1,2,8,8192]{3,2,1,0:T(8,128)S(1)}, u32[]{:S(2)}) copy-start(f32[1,2,8,8192]{3,2,1,0:T(8,128)S(1)} %convert_element_type.19) | copy-start | bytes 1572868
  45.8 19.1 %all-to-all-start.1 = ((f32[64,1,8]{2,1,0:T(1,128)}), f32[64,1,8]{2,1,0:T(1,128)S(1)}, u32[]{:S(2)}, u32[]{:S(2)}) async-start(f32[64,1,8]{2,1,0:T(1,128)} %bitcast.32), calls=%async_computation.1 | async-start | bytes 65536 | tf_op jit(solution)/shard_map/all_to_all | solution.py:121
  52.3 15.2 %collective-permute-start.2 = (f32[4,2,8192]{2,1,0:T(2,128)}, f32[4,2,8192]{2,1,0:T(2,128)S(1)}, u32[]{:S(2)}, u32[]{:S(2)}) collective-permute-start(f32[4,2,8192]{2,1,0:T(2,128)} %get-tuple-element.88), channel_id=1, source_target_pairs={{0,1},{1,2},{2,3},{3,4},{4,5},{5,6},{6,7},{7,8},{8,9},{9,10},{10,1... | collective-permute-start | bytes 786440 | tf_op jit(solution)/shard_map/ppermute | solution.py:23
  55.7 11.9 %collective-permute-start.3 = (f32[4,2,8192]{2,1,0:T(2,128)}, f32[4,2,8192]{2,1,0:T(2,128)S(1)}, u32[]{:S(2)}, u32[]{:S(2)}) collective-permute-start(f32[4,2,8192]{2,1,0:T(2,128)} %get-tuple-element.89), channel_id=1, source_target_pairs={{1,0},{2,1},{3,2},{4,3},{5,4},{6,5},{7,6},{8,7},{9,8},{10,9},{11,1... | collective-permute-start | bytes 786440 | tf_op jit(solution)/shard_map/ppermute | solution.py:25
  67.6 0.7 copy-start.18
  68.3 0.7 copy-start.20
  69.3 2.1 %copy-start = (f32[4,12,8192]{2,1,0:T(8,128)}, f32[4,12,8192]{2,1,0:T(8,128)S(1)}, u32[]{:S(2)}) copy-start(f32[4,12,8192]{2,1,0:T(8,128)S(1)} %pad_maximum_fusion) | copy-start | bytes 4718596
  69.4 2.1 %copy-start.11 = (f32[1,8,8192]{2,1,0:T(8,128)S(1)}, f32[1,8,8192]{2,1,0:T(8,128)}, u32[]{:S(2)}) copy-start(f32[1,8,8192]{2,1,0:T(8,128)} %param.20) | copy-start | bytes 786436
  69.4 2.1 %copy-start.13 = (f32[1,8,8192]{2,1,0:T(8,128)S(1)}, f32[1,8,8192]{2,1,0:T(8,128)}, u32[]{:S(2)}) copy-start(f32[1,8,8192]{2,1,0:T(8,128)} %param.19) | copy-start | bytes 786436
  69.4 2.1 %copy-start.19 = (f32[4,2,8192]{2,1,0:T(2,128)S(1)}, f32[4,2,8192]{2,1,0:T(2,128)}, u32[]{:S(2)}) copy-start(f32[4,2,8192]{2,1,0:T(2,128)} %copy-done.18) | copy-start | bytes 786436
  69.4 2.1 %copy-start.21 = (f32[4,2,8192]{2,1,0:T(2,128)S(1)}, f32[4,2,8192]{2,1,0:T(2,128)}, u32[]{:S(2)}) copy-start(f32[4,2,8192]{2,1,0:T(2,128)} %copy-done.20) | copy-start | bytes 786436
  71.4 1.5 copy-start.7
  73.2 10.4 %collective-permute-start.4 = (f32[4,2,8192]{2,1,0:T(2,128)S(1)}, f32[4,2,8192]{2,1,0:T(2,128)S(1)}, u32[]{:S(2)}, u32[]{:S(2)}) collective-permute-start(f32[4,2,8192]{2,1,0:T(2,128)S(1)} %get-tuple-element.86), channel_id=1, source_target_pairs={{0,1},{1,2},{2,3},{3,4},{4,5},{5,6},{6,7},{7,8},{8,9},{9,10},{10,1... | collective-permute-start | bytes 786440 | tf_op jit(solution)/shard_map/ppermute | solution.py:23
  75.7 9.3 %collective-permute-start.5 = (f32[4,2,8192]{2,1,0:T(2,128)S(1)}, f32[4,2,8192]{2,1,0:T(2,128)S(1)}, u32[]{:S(2)}, u32[]{:S(2)}) collective-permute-start(f32[4,2,8192]{2,1,0:T(2,128)S(1)} %get-tuple-element.87), channel_id=1, source_target_pairs={{1,0},{2,1},{3,2},{4,3},{5,4},{6,5},{7,6},{8,7},{9,8},{10,9},{11,1... | collective-permute-start | bytes 786440 | tf_op jit(solution)/shard_map/ppermute | solution.py:25
  87.4 1.5 copy-start.5
  87.8 1.1 copy-start.3
  98.8 1.4 copy-start.6
  98.8 1.4 copy-start.16
  98.8 1.6 copy-start.17
  103.8 9.7 %collective-permute-start.6 = (f32[3,2,8192]{2,1,0:T(2,128)S(1)}, f32[3,2,8192]{2,1,0:T(2,128)S(1)}, u32[]{:S(2)}, u32[]{:S(2)}) collective-permute-start(f32[3,2,8192]{2,1,0:T(2,128)S(1)} %get-tuple-element.85), channel_id=1, source_target_pairs={{1,0},{2,1},{3,2},{4,3},{5,4},{6,5},{7,6},{8,7},{9,8},{10,9},{11,1... | collective-permute-start | bytes 589832 | tf_op jit(solution)/shard_map/ppermute | solution.py:12
  110.4 10.1 %copy-start.4 = (f32[1,2,8,8192]{3,2,1,0:T(8,128)S(1)}, f32[1,2,8,8192]{3,2,1,0:T(8,128)}, u32[]{:S(2)}) copy-start(f32[1,2,8,8192]{3,2,1,0:T(8,128)} %copy-done.2) | copy-start | bytes 1572868
  110.5 9.8 %collective-permute-start.7 = (f32[3,2,8192]{2,1,0:T(2,128)S(1)}, f32[3,2,8192]{2,1,0:T(2,128)S(1)}, u32[]{:S(2)}, u32[]{:S(2)}) collective-permute-start(f32[3,2,8192]{2,1,0:T(2,128)S(1)} %get-tuple-element.84), channel_id=1, source_target_pairs={{0,1},{1,2},{2,3},{3,4},{4,5},{5,6},{6,7},{7,8},{8,9},{9,10},{10,1... | collective-permute-start | bytes 589832 | tf_op jit(solution)/shard_map/ppermute | solution.py:12
  113.7 7.0 %copy-start.1 = (f32[4,12,8192]{2,1,0:T(8,128)S(1)}, f32[4,12,8192]{2,1,0:T(8,128)}, u32[]{:S(2)}) copy-start(f32[4,12,8192]{2,1,0:T(8,128)} %copy-done) | copy-start | bytes 4718596
  113.7 7.0 %copy-start.8 = (f32[10,8192]{1,0:T(8,128)S(1)}, f32[10,8192]{1,0:T(8,128)}, u32[]{:S(2)}) copy-start(f32[10,8192]{1,0:T(8,128)} %copy-done.7) | copy-start | bytes 983044
  113.7 7.0 %copy-start.14 = (f32[10,8192]{1,0:T(8,128)S(1)}, f32[10,8192]{1,0:T(8,128)}, u32[]{:S(2)}) copy-start(f32[10,8192]{1,0:T(8,128)} %get-tuple-element.75) | copy-start | bytes 983044
  113.7 7.0 %copy-start.15 = (f32[10,8192]{1,0:T(8,128)S(1)}, f32[10,8192]{1,0:T(8,128)}, u32[]{:S(2)}) copy-start(f32[10,8192]{1,0:T(8,128)} %get-tuple-element.109) | copy-start | bytes 983044
  122.4 6.2 %collective-permute-start.8 = (f32[1,2,8192]{2,1,0:T(2,128)S(1)}, f32[1,2,8192]{2,1,0:T(2,128)S(1)}, u32[]{:S(2)}, u32[]{:S(2)}) collective-permute-start(f32[1,2,8192]{2,1,0:T(2,128)S(1)} %get-tuple-element.93), channel_id=1, source_target_pairs={{1,0},{2,1},{3,2},{4,3},{5,4},{6,5},{7,6},{8,7},{9,8},{10,9},{11,1... | collective-permute-start | bytes 196616 | tf_op jit(solution)/shard_map/ppermute | solution.py:12
  124.4 8.3 %collective-permute-start.9 = (f32[1,2,8192]{2,1,0:T(2,128)S(1)}, f32[1,2,8192]{2,1,0:T(2,128)S(1)}, u32[]{:S(2)}, u32[]{:S(2)}) collective-permute-start(f32[1,2,8192]{2,1,0:T(2,128)S(1)} %get-tuple-element.92), channel_id=1, source_target_pairs={{0,1},{1,2},{2,3},{3,4},{4,5},{5,6},{6,7},{7,8},{8,9},{9,10},{10,1... | collective-permute-start | bytes 196616 | tf_op jit(solution)/shard_map/ppermute | solution.py:12
  132.7 3.4 %collective-permute-start.10 = (f32[8,8192]{1,0:T(8,128)S(1)}, f32[8,8192]{1,0:T(8,128)S(1)}, u32[]{:S(2)}, u32[]{:S(2)}) collective-permute-start(f32[8,8192]{1,0:T(8,128)S(1)} %fusion.42), channel_id=1, source_target_pairs={{0,64},{64,0},{128,192},{192,128},{256,320},{320,256},{384,448},{4... | collective-permute-start | bytes 786440 | tf_op jit(solution)/shard_map/ppermute | solution.py:161
  136.2 10.2 %collective-permute-start.11 = (f32[8,8192]{1,0:T(8,128)S(1)}, f32[8,8192]{1,0:T(8,128)S(1)}, u32[]{:S(2)}, u32[]{:S(2)}) collective-permute-start(f32[8,8192]{1,0:T(8,128)S(1)} %add.191), channel_id=1, source_target_pairs={{0,128},{64,192},{128,0},{192,64},{256,384},{320,448},{384,256},{4... | collective-permute-start | bytes 786440 | tf_op jit(solution)/shard_map/ppermute | solution.py:161
  146.5 10.9 %collective-permute-start.12 = (f32[8,8192]{1,0:T(8,128)S(1)}, f32[8,8192]{1,0:T(8,128)S(1)}, u32[]{:S(2)}, u32[]{:S(2)}) collective-permute-start(f32[8,8192]{1,0:T(8,128)S(1)} %add.192), channel_id=1, source_target_pairs={{0,256},{64,320},{128,384},{192,448},{256,0},{320,64},{384,128},{4... | collective-permute-start | bytes 786440 | tf_op jit(solution)/shard_map/ppermute | solution.py:161
